TPU v7x, 256 devices: a whole 4x4x8 slice. The times are simulated.
256 devices in a mesh: obs: 8 (over z_hi, core), horiz: 32 (over y, z_lo, x).
Axes of the slice: x: 4, y: 4, z: 8 (z_hi: 4, z_lo: 2; z = z_hi * 2 + z_lo), core: 2. Of those that a mesh axis runs over, the one named last changes fastest.
Arguments:
- control: float32 [128, 64, 4096], P(None, 'obs', 'horiz'), may hold values from -6 to 6
- spread: float32 [128, 64, 4096], P(None, 'obs', 'horiz'), may hold values from 0.3 to 3
- vert_root: float32 [128, 128], replicated, as said below
- wind_lon: float32 [128, 64, 4096], P('horiz', 'obs'), may hold values from -0.45 to 0.45
- wind_lat: float32 [128, 64, 4096], P('horiz', 'obs'), may hold values from -0.45 to 0.45
- obs_dest: int32 [262144, 1], P(('obs', 'horiz')), may hold values from 0 to 31; in each aligned block of 1024 rows (0 to 1023, 1024 to 2047, ...) at most 64 rows name the same one
- obs_cells: int32 [4, 262144], P(None, ('obs', 'horiz')), may hold values from 0 to 131071
- obs_time: int32 [262144], P(('obs', 'horiz')), may hold values from 0 to 4
- obs_value: float32 [262144], P(('obs', 'horiz')), may hold values from -6 to 6
- obs_weight: float32 [4, 262144], P(None, ('obs', 'horiz')), may hold values from 0 to 1
- obs_rinv: float32 [262144], P(('obs', 'horiz')), may hold values from 0.3 to 3
Outputs:
- gradient: float32 [128, 64, 4096], P(None, 'obs', 'horiz')
- departure: float32 [262144], P(('obs', 'horiz'))
Inputs may be any that keep to these rules, and one draw needn't show every extreme that they name: `obs_dest`: in the rows of one device at most 64 observations name the same level group, a bound that some block reaches. `obs_cells`: cell index within the owner's block of 128 / 32 levels, 8 rows and 4096 longitudes, flattened in that order. `vert_root`: zero beyond 12 places from the diagonal; diagonal entries from 1 to 1.5.
All inputs are finite; a program needn't handle non-finite values.
Results may differ from a plain program's by a relative error of at most 0.00012.
Values sent between devices are 32-bit elements; how exact they have to be, the bound alone decides.
A program may use at most 64 MiB of HBM per device.

v0:
```python
import jax
import jax.numpy as jnp
from jax import lax
from jax.sharding import PartitionSpec as P

NT = 4
CAP = 64


def padded_2(cells, sides, width):
    for axis, dim in sides:
        count = lax.axis_size(axis)
        ends = count - 1
        head = lax.slice_in_dim(cells, 0, width, axis=dim)
        tail = lax.slice_in_dim(cells, cells.shape[dim] - width, cells.shape[dim], axis=dim)
        cells = jnp.concatenate(
            [
                lax.ppermute(tail, axis, [(i, (i + 1) % count) for i in range(ends)]),
                cells,
                lax.ppermute(head, axis, [((i + 1) % count, i) for i in range(ends)]),
            ],
            axis=dim,
        )
    return cells


def advance(current, west_cells, east_cells, south_rows, north_rows, wind_u, wind_v):
    up_lon = jnp.maximum(wind_u, 0.0)
    down_lon = jnp.minimum(wind_u, 0.0)
    up_lat = jnp.maximum(wind_v, 0.0)
    down_lat = jnp.minimum(wind_v, 0.0)
    return (
        current
        - up_lon * (current - west_cells)
        - down_lon * (east_cells - current)
        - up_lat * (current - south_rows)
        - down_lat * (north_rows - current)
    )


def adjoint_terms(adjoint_now, wind_u, wind_v):
    up_lon = jnp.maximum(wind_u, 0.0)
    down_lon = jnp.minimum(wind_u, 0.0)
    up_lat = jnp.maximum(wind_v, 0.0)
    down_lat = jnp.minimum(wind_v, 0.0)
    base = (1.0 - up_lon + down_lon - up_lat + down_lat) * adjoint_now
    base = (
        base
        + jnp.roll(up_lon * adjoint_now, -1, axis=2)
        - jnp.roll(down_lon * adjoint_now, 1, axis=2)
    )
    return (base, up_lat * adjoint_now, down_lat * adjoint_now)


def per_device(
    control,
    spread,
    vert_root,
    wind_lon,
    wind_lat,
    obs_dest,
    obs_cells,
    obs_time,
    obs_value,
    obs_weight,
    obs_rinv,
):
    levels_all = control.shape[0]
    groups = lax.axis_size("horiz")
    increment = spread * jnp.dot(
        vert_root,
        control.reshape(levels_all, -1),
        precision=lax.Precision.HIGHEST,
        preferred_element_type=jnp.float32,
    ).reshape(control.shape)
    field = lax.all_to_all(increment, "horiz", split_axis=0, concat_axis=2, tiled=True)
    level_count, lat_rows, lon_cells = field.shape
    states = [field]
    current = field
    for tick_index in range(NT):
        padded = padded_2(current, (("obs", 1),), 1)
        current = advance(
            current,
            jnp.roll(current, 1, axis=2),
            jnp.roll(current, -1, axis=2),
            padded[:, :-2],
            padded[:, 2:],
            wind_lon,
            wind_lat,
        )
        states.append(current)
    owner_ids = obs_dest[:, 0]
    onehot = (owner_ids[:, None] == jnp.arange(groups, dtype=jnp.int32)[None, :]).astype(jnp.int32)
    before = jnp.cumsum(onehot, axis=0) - onehot
    slot_ids = jnp.sum(before * onehot, axis=1)
    placed = owner_ids * CAP + slot_ids
    slot_hit = (placed[:, None] == jnp.arange(groups * CAP, dtype=jnp.int32)[None, :]).astype(
        jnp.float32
    )
    reals = jnp.concatenate([obs_value[None, :], obs_rinv[None, :], obs_weight], axis=0)
    integers = jnp.concatenate([obs_time[None, :], obs_cells], axis=0).astype(jnp.float32)
    real_buffer = jnp.dot(
        reals, slot_hit, precision=lax.Precision.HIGHEST, preferred_element_type=jnp.float32
    ).reshape(6, groups, CAP)
    int_buffer = (
        jnp.dot(
            integers, slot_hit, precision=lax.Precision.HIGHEST, preferred_element_type=jnp.float32
        )
        .astype(jnp.int32)
        .reshape(5, groups, CAP)
    )
    got_real, got_int = (
        lax.all_to_all(real_buffer, "horiz", split_axis=1, concat_axis=1, tiled=True),
        lax.all_to_all(int_buffer, "horiz", split_axis=1, concat_axis=1, tiled=True),
    )
    got_real = got_real.reshape(6, groups * CAP)
    got_int = got_int.reshape(5, groups * CAP)
    states_rows = jnp.stack(states).reshape(-1, 128)
    block_size = level_count * lat_rows * lon_cells
    where_ids = got_int[0][None, :] * block_size + got_int[1:5]
    row_ids = where_ids // 128
    lane_ids = where_ids % 128
    lane_hit = (lane_ids[:, :, None] == jnp.arange(128, dtype=jnp.int32)[None, None, :]).astype(
        jnp.float32
    )
    picked = jnp.sum(states_rows[row_ids] * lane_hit, axis=2)
    hx = jnp.sum(got_real[2:6] * picked, axis=0)
    owner_dep = got_real[1] * (hx - got_real[0])
    spread_rows = (lane_hit * (got_real[2:6] * owner_dep[None, :])[:, :, None]).reshape(-1, 128)
    forcing = jnp.zeros(states_rows.shape, jnp.float32).at[row_ids.reshape(-1)].add(spread_rows)
    forcing = forcing.reshape(NT + 1, level_count, lat_rows, lon_cells)
    returned = lax.all_to_all(
        owner_dep.reshape(groups, CAP), "horiz", split_axis=0, concat_axis=0, tiled=True
    )
    departure = jnp.dot(
        slot_hit,
        returned.reshape(-1),
        precision=lax.Precision.HIGHEST,
        preferred_element_type=jnp.float32,
    )
    adjoint_now = forcing[NT]
    for tick_index in range(NT - 1, -1, -1):
        base, plus_flux, minus_flux = adjoint_terms(adjoint_now, wind_lon, wind_lat)
        rims = padded_2(jnp.stack([plus_flux, minus_flux]), (("obs", 2),), 1)
        adjoint_now = base + rims[0][:, 2:] - rims[1][:, :-2] + forcing[tick_index]
    column = lax.all_to_all(adjoint_now, "horiz", split_axis=2, concat_axis=0, tiled=True)
    weighted = (spread * column).reshape(levels_all, -1)
    gradient = control + jnp.dot(
        vert_root.T, weighted, precision=lax.Precision.HIGHEST, preferred_element_type=jnp.float32
    ).reshape(control.shape)
    return (gradient, departure)


def solution(mesh):
    in_specs = (
        P(None, "obs", "horiz"),
        P(None, "obs", "horiz"),
        P(),
        P("horiz", "obs", None),
        P("horiz", "obs", None),
        P(("obs", "horiz"), None),
        P(None, ("obs", "horiz")),
        P(("obs", "horiz")),
        P(("obs", "horiz")),
        P(None, ("obs", "horiz")),
        P(("obs", "horiz")),
    )
    out_specs = (P(None, "obs", "horiz"), P(("obs", "horiz")))
    return jax.shard_map(
        per_device, mesh=mesh, in_specs=in_specs, out_specs=out_specs, check_vma=False
    )
```

profile of v0, /device:TPU:67, one launch (start us, length us, event | category | flops | bytes accessed | tf_op | source)
XLA Modules:
  0.0 335.4 jit_solution(12801752705379913154)
XLA Ops:
  1.4 9.0 %reduce-window.6 = s32[32,8,128]{2,1,0:T(8,128)S(1)} reduce-window(s32[32,8,128]{2,1,0:T(8,128)S(1)} %fusion.69, s32[]{:T(128)} %constant.42.clone.1), window={size=1x1x128 pad=0_0x0_0x127_0}, to_apply=%region_0.1 | reduce-window | flops 4161536 | bytes 262148 | tf_op jit(solution)/shard_map/reduce-window
  16.7 8.4 %all-to-all-start = ((s32[32,1,320]{2,1,0:T(1,128)}), s32[32,1,320]{2,1,0:T(1,128)S(1)}, u32[]{:S(2)}, u32[]{:S(2)}) async-start(s32[32,1,320]{2,1,0:T(1,128)} %reshape.382), calls=%async_computation | async-start | bytes 98304 | tf_op jit(solution)/shard_map/all_to_all | solution.py:114
  31.5 7.1 %all-to-all-start.1 = ((f32[32,1,384]{2,1,0:T(1,128)}), f32[32,1,384]{2,1,0:T(1,128)S(1)}, u32[]{:S(2)}, u32[]{:S(2)}) async-start(f32[32,1,384]{2,1,0:T(1,128)} %reshape.384), calls=%async_computation.1 | async-start | bytes 98304 | tf_op jit(solution)/shard_map/all_to_all | solution.py:113
  40.4 4.6 %all-to-all-done.1 = f32[32,1,384]{2,1,0:T(1,128)S(1)} async-done(((f32[32,1,384]{2,1,0:T(1,128)}), f32[32,1,384]{2,1,0:T(1,128)S(1)}, u32[]{:S(2)}, u32[]{:S(2)}) %all-to-all-start.1) | async-done | bytes 49184 | tf_op jit(solution)/shard_map/all_to_all | solution.py:113
  45.0 4.7 %all-to-all-start.2 = ((f32[128,8,128]{2,1,0:T(8,128)}), f32[128,8,128]{2,1,0:T(8,128)S(1)}, u32[]{:S(2)}, u32[]{:S(2)}) async-start(f32[128,8,128]{2,1,0:T(8,128)} %copy.56), calls=%async_computation.2 | async-start | bytes 1048576 | tf_op jit(solution)/shard_map/all_to_all | solution.py:76
  51.8 6.6 %all-to-all-done.2 = f32[128,8,128]{2,1,0:T(8,128)S(1)} async-done(((f32[128,8,128]{2,1,0:T(8,128)}), f32[128,8,128]{2,1,0:T(8,128)S(1)}, u32[]{:S(2)}, u32[]{:S(2)}) %all-to-all-start.2) | async-done | bytes 524320 | tf_op jit(solution)/shard_map/all_to_all | solution.py:76
  59.6 8.8 %collective-permute-start = (f32[4,1,4096]{2,1,0:T(1,128)S(1)}, f32[4,1,4096]{2,1,0:T(1,128)S(1)}, u32[]{:S(2)}, u32[]{:S(2)}) collective-permute-start(f32[4,1,4096]{2,1,0:T(1,128)S(1)} %get-tuple-element.73), channel_id=1, source_target_pairs={{0,32},{32,64},{64,96},{96,128},{128,160},{160,192},{192,224},{1,3... | collective-permute-start | bytes 196616 | tf_op jit(solution)/shard_map/ppermute | solution.py:18
  70.4 6.4 %collective-permute-done.1 = f32[4,1,4096]{2,1,0:T(1,128)S(1)} collective-permute-done((f32[4,1,4096]{2,1,0:T(1,128)S(1)}, f32[4,1,4096]{2,1,0:T(1,128)S(1)}, u32[]{:S(2)}, u32[]{:S(2)}) %collective-permute-start.1) | collective-permute-done | bytes 65568 | tf_op jit(solution)/shard_map/ppermute | solution.py:20
  83.0 5.6 %collective-permute-done.3 = f32[4,1,4096]{2,1,0:T(1,128)S(1)} collective-permute-done((f32[4,1,4096]{2,1,0:T(1,128)S(1)}, f32[4,1,4096]{2,1,0:T(1,128)S(1)}, u32[]{:S(2)}, u32[]{:S(2)}) %collective-permute-start.3) | collective-permute-done | bytes 65568 | tf_op jit(solution)/shard_map/ppermute | solution.py:20
  94.7 5.3 %collective-permute-done.5 = f32[4,1,4096]{2,1,0:T(1,128)S(1)} collective-permute-done((f32[4,1,4096]{2,1,0:T(1,128)S(1)}, f32[4,1,4096]{2,1,0:T(1,128)S(1)}, u32[]{:S(2)}, u32[]{:S(2)}) %collective-permute-start.5) | collective-permute-done | bytes 65568 | tf_op jit(solution)/shard_map/ppermute | solution.py:20
  105.9 5.2 %collective-permute-done.7 = f32[4,1,4096]{2,1,0:T(1,128)S(1)} collective-permute-done((f32[4,1,4096]{2,1,0:T(1,128)S(1)}, f32[4,1,4096]{2,1,0:T(1,128)S(1)}, u32[]{:S(2)}, u32[]{:S(2)}) %collective-permute-start.7) | collective-permute-done | bytes 65568 | tf_op jit(solution)/shard_map/ppermute | solution.py:20
  115.0 27.8 %gather_fusion = f32[8192,128]{1,0:T(8,128)} fusion(f32[5120,128]{1,0:T(8,128)S(1)} %reshape.334, s32[8192]{0:T(1024)S(1)} %broadcast_clamp_fusion), kind=kCustom, calls=%fused_computation | custom fusion | bytes 8421376 | tf_op jit(solution)/shard_map/gather | solution.py:126
  142.8 4.4 %select_reduce_fusion = f32[4,2048]{1,0:T(4,128)S(1)} fusion(f32[4,2048,128]{2,1,0:T(8,128)} %bitcast.147, s32[4,2048]{1,0:T(4,128)S(1)} %get-tuple-element.80), kind=kLoop, calls=%fused_computation.8 | loop fusion | flops 3137536 | bytes 4259840 | tf_op jit(solution)/shard_map/reduce_sum | solution.py:126
  147.6 57.0 %scatter_custom_fusion = f32[5120,128]{1,0:T(8,128)} fusion(s32[8192]{0:T(1024)S(1)} %bitcast.179, f32[]{:T(128)} %constant.40.clone.1, f32[8192]{0:T(1024)S(1)} %mul.212, s32[8192]{0:T(1024)S(1)} %add_select_fusion.2), kind=kCustom, calls=%fused_computation.6 | custom fusion | flops 3145728 | bytes 2688000 | tf_op jit(solution)/shard_map/scatter-add | solution.py:130
  242.1 3.7 %collective-permute-start.12 = (f32[2,4,1,4096]{3,2,1,0:T(1,128)}, f32[2,4,1,4096]{3,2,1,0:T(1,128)}, u32[]{:S(2)}, u32[]{:S(2)}) collective-permute-start(f32[2,4,1,4096]{3,2,1,0:T(1,128)} %get-tuple-element.32), channel_id=1, source_target_pairs={{0,32},{32,64},{64,96},{96,128},{128,160},{160,192},{192,224},{1,3... | collective-permute-start | bytes 393224 | tf_op jit(solution)/shard_map/ppermute | solution.py:18
  259.9 3.8 %collective-permute-start.14 = (f32[2,4,1,4096]{3,2,1,0:T(1,128)}, f32[2,4,1,4096]{3,2,1,0:T(1,128)}, u32[]{:S(2)}, u32[]{:S(2)}) collective-permute-start(f32[2,4,1,4096]{3,2,1,0:T(1,128)} %get-tuple-element.28), channel_id=1, source_target_pairs={{0,32},{32,64},{64,96},{96,128},{128,160},{160,192},{192,224},{1,3... | collective-permute-start | bytes 393224 | tf_op jit(solution)/shard_map/ppermute | solution.py:18
  266.2 4.5 %all-to-all-start.4 = ((f32[32,1,64]{2,1,0:T(1,128)}), f32[32,1,64]{2,1,0:T(1,128)S(1)}, u32[]{:S(2)}, u32[]{:S(2)}) async-start(f32[32,1,64]{2,1,0:T(1,128)} %bitcast.49), calls=%async_computation.4 | async-start | bytes 32768 | tf_op jit(solution)/shard_map/all_to_all | solution.py:132
  276.4 5.9 %copy.59 = f32[4,8,4096]{1,0,2:T(4,128)} copy(f32[4,8,4096]{2,1,0:T(8,128)S(1)} %fusion.16) | data formatting | bytes 1048576 | tf_op jit(solution)/shard_map/add | solution.py:145
  282.3 12.1 %reshape.386 = f32[32,1,4096]{2,1,0:T(1,128)} reshape(f32[4096,4,8]{2,1,0:T(4,128)} %bitcast.145) | data formatting | bytes 1048576
  294.4 7.7 %all-to-all-start.3 = ((f32[32,1,4096]{2,1,0:T(1,128)}), f32[32,1,4096]{2,1,0:T(1,128)S(1)}, u32[]{:S(2)}, u32[]{:S(2)}) async-start(f32[32,1,4096]{2,1,0:T(1,128)} %reshape.386), calls=%async_computation.3 | async-start | bytes 1048576 | tf_op jit(solution)/shard_map/all_to_all | solution.py:146
  303.5 4.4 %fusion = f32[1,1024]{1,0:T(1,128)} fusion(f32[2048,1]{0,1:T(1,128)S(1)} %reshape.356, s32[1024]{0:T(1024)S(1)} %bitcast.184), kind=kOutput, calls=%fused_computation.3 | convolution fusion | flops 27262976 | bytes 16384 | tf_op jit(solution)/shard_map/dot_general | solution.py:135
  307.9 5.4 %all-to-all-done.3 = f32[32,1,4096]{2,1,0:T(1,128)S(1)} async-done(((f32[32,1,4096]{2,1,0:T(1,128)}), f32[32,1,4096]{2,1,0:T(1,128)S(1)}, u32[]{:S(2)}, u32[]{:S(2)}) %all-to-all-start.3) | async-done | bytes 524320 | tf_op jit(solution)/shard_map/all_to_all | solution.py:146
  315.1 11.4 %reshape.387 = f32[4096,4,8]{2,1,0:T(4,128)} reshape(f32[32,4096]{1,0:T(8,128)S(1)} %reduce.15) | data formatting | bytes 1048576
  326.5 6.6 %copy.60 = f32[32,4,8,128]{3,2,1,0:T(8,128)S(1)} copy(f32[32,4,8,128]{2,1,3,0:T(4,128)} %bitcast.146) | data formatting | bytes 1048576 | tf_op jit(solution)/shard_map/all_to_all | solution.py:146
  (189 shorter events, 107.5 us)
Async XLA Ops:
  0.6 24.8 %copy-start = (f32[128,128]{1,0:T(8,128)S(1)}, f32[128,128]{1,0:T(8,128)}, u32[]{:S(2)}) copy-start(f32[128,128]{1,0:T(8,128)} %param.13) | copy-start | bytes 196612
  16.7 14.8 %all-to-all-start = ((s32[32,1,320]{2,1,0:T(1,128)}), s32[32,1,320]{2,1,0:T(1,128)S(1)}, u32[]{:S(2)}, u32[]{:S(2)}) async-start(s32[32,1,320]{2,1,0:T(1,128)} %reshape.382), calls=%async_computation | async-start | bytes 98304 | tf_op jit(solution)/shard_map/all_to_all | solution.py:114
  31.5 13.5 %all-to-all-start.1 = ((f32[32,1,384]{2,1,0:T(1,128)}), f32[32,1,384]{2,1,0:T(1,128)S(1)}, u32[]{:S(2)}, u32[]{:S(2)}) async-start(f32[32,1,384]{2,1,0:T(1,128)} %reshape.384), calls=%async_computation.1 | async-start | bytes 98304 | tf_op jit(solution)/shard_map/all_to_all | solution.py:113
  45.0 13.4 %all-to-all-start.2 = ((f32[128,8,128]{2,1,0:T(8,128)}), f32[128,8,128]{2,1,0:T(8,128)S(1)}, u32[]{:S(2)}, u32[]{:S(2)}) async-start(f32[128,8,128]{2,1,0:T(8,128)} %copy.56), calls=%async_computation.2 | async-start | bytes 1048576 | tf_op jit(solution)/shard_map/all_to_all | solution.py:76
  50.1 26.7 %copy-start.1 = (f32[4,8,4096]{2,1,0:T(8,128)S(1)}, f32[4,8,4096]{2,1,0:T(8,128)}, u32[]{:S(2)}) copy-start(f32[4,8,4096]{2,1,0:T(8,128)} %param.14) | copy-start | bytes 1572868
  50.2 26.7 %copy-start.2 = (f32[4,8,4096]{2,1,0:T(8,128)S(1)}, f32[4,8,4096]{2,1,0:T(8,128)}, u32[]{:S(2)}) copy-start(f32[4,8,4096]{2,1,0:T(8,128)} %param.15) | copy-start | bytes 1572868
  59.6 10.8 %collective-permute-start = (f32[4,1,4096]{2,1,0:T(1,128)S(1)}, f32[4,1,4096]{2,1,0:T(1,128)S(1)}, u32[]{:S(2)}, u32[]{:S(2)}) collective-permute-start(f32[4,1,4096]{2,1,0:T(1,128)S(1)} %get-tuple-element.73), channel_id=1, source_target_pairs={{0,32},{32,64},{64,96},{96,128},{128,160},{160,192},{192,224},{1,3... | collective-permute-start | bytes 196616 | tf_op jit(solution)/shard_map/ppermute | solution.py:18
  68.4 8.4 %collective-permute-start.1 = (f32[4,1,4096]{2,1,0:T(1,128)S(1)}, f32[4,1,4096]{2,1,0:T(1,128)S(1)}, u32[]{:S(2)}, u32[]{:S(2)}) collective-permute-start(f32[4,1,4096]{2,1,0:T(1,128)S(1)} %get-tuple-element.74), channel_id=1, source_target_pairs={{32,0},{64,32},{96,64},{128,96},{160,128},{192,160},{224,192},{33,... | collective-permute-start | bytes 196616 | tf_op jit(solution)/shard_map/ppermute | solution.py:20
  78.4 4.6 %collective-permute-start.2 = (f32[4,1,4096]{2,1,0:T(1,128)S(1)}, f32[4,1,4096]{2,1,0:T(1,128)S(1)}, u32[]{:S(2)}, u32[]{:S(2)}) collective-permute-start(f32[4,1,4096]{2,1,0:T(1,128)S(1)} %get-tuple-element.67), channel_id=1, source_target_pairs={{0,32},{32,64},{64,96},{96,128},{128,160},{160,192},{192,224},{1,3... | collective-permute-start | bytes 196616 | tf_op jit(solution)/shard_map/ppermute | solution.py:18
  80.4 8.3 %collective-permute-start.3 = (f32[4,1,4096]{2,1,0:T(1,128)S(1)}, f32[4,1,4096]{2,1,0:T(1,128)S(1)}, u32[]{:S(2)}, u32[]{:S(2)}) collective-permute-start(f32[4,1,4096]{2,1,0:T(1,128)S(1)} %get-tuple-element.68), channel_id=1, source_target_pairs={{32,0},{64,32},{96,64},{128,96},{160,128},{192,160},{224,192},{33,... | collective-permute-start | bytes 196616 | tf_op jit(solution)/shard_map/ppermute | solution.py:20
  90.3 4.4 %collective-permute-start.4 = (f32[4,1,4096]{2,1,0:T(1,128)S(1)}, f32[4,1,4096]{2,1,0:T(1,128)S(1)}, u32[]{:S(2)}, u32[]{:S(2)}) collective-permute-start(f32[4,1,4096]{2,1,0:T(1,128)S(1)} %get-tuple-element.61), channel_id=1, source_target_pairs={{0,32},{32,64},{64,96},{96,128},{128,160},{160,192},{192,224},{1,3... | collective-permute-start | bytes 196616 | tf_op jit(solution)/shard_map/ppermute | solution.py:18
  92.2 7.8 %collective-permute-start.5 = (f32[4,1,4096]{2,1,0:T(1,128)S(1)}, f32[4,1,4096]{2,1,0:T(1,128)S(1)}, u32[]{:S(2)}, u32[]{:S(2)}) collective-permute-start(f32[4,1,4096]{2,1,0:T(1,128)S(1)} %get-tuple-element.62), channel_id=1, source_target_pairs={{32,0},{64,32},{96,64},{128,96},{160,128},{192,160},{224,192},{33,... | collective-permute-start | bytes 196616 | tf_op jit(solution)/shard_map/ppermute | solution.py:20
  101.5 4.4 %collective-permute-start.6 = (f32[4,1,4096]{2,1,0:T(1,128)S(1)}, f32[4,1,4096]{2,1,0:T(1,128)S(1)}, u32[]{:S(2)}, u32[]{:S(2)}) collective-permute-start(f32[4,1,4096]{2,1,0:T(1,128)S(1)} %get-tuple-element.55), channel_id=1, source_target_pairs={{0,32},{32,64},{64,96},{96,128},{128,160},{160,192},{192,224},{1,3... | collective-permute-start | bytes 196616 | tf_op jit(solution)/shard_map/ppermute | solution.py:18
  103.4 7.7 %collective-permute-start.7 = (f32[4,1,4096]{2,1,0:T(1,128)S(1)}, f32[4,1,4096]{2,1,0:T(1,128)S(1)}, u32[]{:S(2)}, u32[]{:S(2)}) collective-permute-start(f32[4,1,4096]{2,1,0:T(1,128)S(1)} %get-tuple-element.56), channel_id=1, source_target_pairs={{32,0},{64,32},{96,64},{128,96},{160,128},{192,160},{224,192},{33,... | collective-permute-start | bytes 196616 | tf_op jit(solution)/shard_map/ppermute | solution.py:20
  208.7 7.4 %collective-permute-start.8 = (f32[2,4,1,4096]{3,2,1,0:T(1,128)}, f32[2,4,1,4096]{3,2,1,0:T(1,128)}, u32[]{:S(2)}, u32[]{:S(2)}) collective-permute-start(f32[2,4,1,4096]{3,2,1,0:T(1,128)} %get-tuple-element.42), channel_id=1, source_target_pairs={{0,32},{32,64},{64,96},{96,128},{128,160},{160,192},{192,224},{1,3... | collective-permute-start | bytes 393224 | tf_op jit(solution)/shard_map/ppermute | solution.py:18
  210.7 8.6 %collective-permute-start.9 = (f32[2,4,1,4096]{3,2,1,0:T(1,128)S(1)}, f32[2,4,1,4096]{3,2,1,0:T(1,128)}, u32[]{:S(2)}, u32[]{:S(2)}) collective-permute-start(f32[2,4,1,4096]{3,2,1,0:T(1,128)S(1)} %get-tuple-element.43), channel_id=1, source_target_pairs={{32,0},{64,32},{96,64},{128,96},{160,128},{192,160},{224,192},{33,... | collective-permute-start | bytes 393224 | tf_op jit(solution)/shard_map/ppermute | solution.py:20
  225.9 9.0 %collective-permute-start.10 = (f32[2,4,1,4096]{3,2,1,0:T(1,128)}, f32[2,4,1,4096]{3,2,1,0:T(1,128)}, u32[]{:S(2)}, u32[]{:S(2)}) collective-permute-start(f32[2,4,1,4096]{3,2,1,0:T(1,128)} %get-tuple-element.36), channel_id=1, source_target_pairs={{0,32},{32,64},{64,96},{96,128},{128,160},{160,192},{192,224},{1,3... | collective-permute-start | bytes 393224 | tf_op jit(solution)/shard_map/ppermute | solution.py:18
  228.0 8.6 %collective-permute-start.11 = (f32[2,4,1,4096]{3,2,1,0:T(1,128)S(1)}, f32[2,4,1,4096]{3,2,1,0:T(1,128)}, u32[]{:S(2)}, u32[]{:S(2)}) collective-permute-start(f32[2,4,1,4096]{3,2,1,0:T(1,128)S(1)} %get-tuple-element.37), channel_id=1, source_target_pairs={{32,0},{64,32},{96,64},{128,96},{160,128},{192,160},{224,192},{33,... | collective-permute-start | bytes 393224 | tf_op jit(solution)/shard_map/ppermute | solution.py:20
  242.1 10.4 %collective-permute-start.12 = (f32[2,4,1,4096]{3,2,1,0:T(1,128)}, f32[2,4,1,4096]{3,2,1,0:T(1,128)}, u32[]{:S(2)}, u32[]{:S(2)}) collective-permute-start(f32[2,4,1,4096]{3,2,1,0:T(1,128)} %get-tuple-element.32), channel_id=1, source_target_pairs={{0,32},{32,64},{64,96},{96,128},{128,160},{160,192},{192,224},{1,3... | collective-permute-start | bytes 393224 | tf_op jit(solution)/shard_map/ppermute | solution.py:18
  245.8 8.6 %collective-permute-start.13 = (f32[2,4,1,4096]{3,2,1,0:T(1,128)S(1)}, f32[2,4,1,4096]{3,2,1,0:T(1,128)}, u32[]{:S(2)}, u32[]{:S(2)}) collective-permute-start(f32[2,4,1,4096]{3,2,1,0:T(1,128)S(1)} %get-tuple-element.33), channel_id=1, source_target_pairs={{32,0},{64,32},{96,64},{128,96},{160,128},{192,160},{224,192},{33,... | collective-permute-start | bytes 393224 | tf_op jit(solution)/shard_map/ppermute | solution.py:20
  259.9 13.8 %collective-permute-start.14 = (f32[2,4,1,4096]{3,2,1,0:T(1,128)}, f32[2,4,1,4096]{3,2,1,0:T(1,128)}, u32[]{:S(2)}, u32[]{:S(2)}) collective-permute-start(f32[2,4,1,4096]{3,2,1,0:T(1,128)} %get-tuple-element.28), channel_id=1, source_target_pairs={{0,32},{32,64},{64,96},{96,128},{128,160},{160,192},{192,224},{1,3... | collective-permute-start | bytes 393224 | tf_op jit(solution)/shard_map/ppermute | solution.py:18
  263.7 10.0 %collective-permute-start.15 = (f32[2,4,1,4096]{3,2,1,0:T(1,128)S(1)}, f32[2,4,1,4096]{3,2,1,0:T(1,128)}, u32[]{:S(2)}, u32[]{:S(2)}) collective-permute-start(f32[2,4,1,4096]{3,2,1,0:T(1,128)S(1)} %get-tuple-element.29), channel_id=1, source_target_pairs={{32,0},{64,32},{96,64},{128,96},{160,128},{192,160},{224,192},{33,... | collective-permute-start | bytes 393224 | tf_op jit(solution)/shard_map/ppermute | solution.py:20
  266.2 28.2 %all-to-all-start.4 = ((f32[32,1,64]{2,1,0:T(1,128)}), f32[32,1,64]{2,1,0:T(1,128)S(1)}, u32[]{:S(2)}, u32[]{:S(2)}) async-start(f32[32,1,64]{2,1,0:T(1,128)} %bitcast.49), calls=%async_computation.4 | async-start | bytes 32768 | tf_op jit(solution)/shard_map/all_to_all | solution.py:132
  294.4 18.8 %all-to-all-start.3 = ((f32[32,1,4096]{2,1,0:T(1,128)}), f32[32,1,4096]{2,1,0:T(1,128)S(1)}, u32[]{:S(2)}, u32[]{:S(2)}) async-start(f32[32,1,4096]{2,1,0:T(1,128)} %reshape.386), calls=%async_computation.3 | async-start | bytes 1048576 | tf_op jit(solution)/shard_map/all_to_all | solution.py:146
  (18 other events, 130.6 us)
where the time goes:
time: 337 us; the launch traced here: 335 us
  other arithmetic  100 us (30%)
  local copies, waits for them, and re-layouts  98.3 us (29%)
  starting transfers between devices  76.3 us (23%)
  waiting for transfers between devices  46.6 us (14%)
  matrix products  12.3 us (4%)
    scatter-add x1, other arithmetic, per_device(): jnp.zeros(states_rows.shape, jnp.float32).at[row_ids.reshape(-1)]  57 us
    unnamed x52, local copies, waits for them, and re-layouts  30 us
    ppermute x8, waiting for transfers between devices, padded_2(): lax.ppermute(head, axis, [((i + 1) % count, i) for i in range(ends)])  29.4 us
    gather x1, local copies, waits for them, and re-layouts, per_device(): picked = jnp.sum(states_rows[row_ids] * lane_hit, axis=2)  27.8 us
    ppermute x8, starting transfers between devices, padded_2(): lax.ppermute(tail, axis, [(i, (i + 1) % count) for i in range(ends)])  26.1 us
    ppermute x8, starting transfers between devices, padded_2(): lax.ppermute(head, axis, [((i + 1) % count, i) for i in range(ends)])  17.8 us
    another operation x3, other arithmetic  9.15 us
    squeeze x8, local copies, waits for them, and re-layouts, per_device(): adjoint_now = base + rims[0][:, 2:] - rims[1][:, :-2] + forcing[tick_index]  8.49 us
  transfers between devices with their start and end apart: 21, of which 11 were waited for; matrix products, arithmetic and copies ran while one was open for 15% of the time, Pallas kernels for 0%

commit v1 on v0

v1 whole, which is shorter than its diff:
```python
import jax
import jax.numpy as jnp
from jax import lax
from jax.experimental import pallas as pl
from jax.experimental.pallas import tpu as pltpu
from jax.sharding import PartitionSpec as P

NT = 4
CAP = 64
GROUPS = 32
BANDS = 8
LEVELS = 4
TILES = 32
ROWS = TILES * 8
ACCS = 8
MESH = pl.DeviceIdType.MESH
F32 = jnp.float32
I32 = jnp.int32
BF16 = jnp.bfloat16


def in_vmem():
    return pl.BlockSpec(memory_space=pltpu.VMEM)


def in_hbm():
    return pl.BlockSpec(memory_space=pltpu.HBM)


def fetches(sources, targets, sems):
    return [
        pltpu.make_async_copy(source, target, sems.at[index])
        for index, (source, target) in enumerate(zip(sources, targets))
    ]


def split_three(x):
    high = x.astype(BF16)
    rest = x - high.astype(F32)
    middle = rest.astype(BF16)
    low = (rest - middle.astype(F32)).astype(BF16)
    return high, middle, low


def greet(band, group):
    barrier = pltpu.get_barrier_semaphore()

    def peer(step, carry):
        other = lax.rem(group + step, GROUPS)
        pl.semaphore_signal(barrier, inc=1, device_id=(band, other), device_id_type=MESH)
        return carry

    lax.fori_loop(1, GROUPS, peer, 0)

    @pl.when(band > 0)
    def _():
        pl.semaphore_signal(barrier, inc=1, device_id=(band - 1, group), device_id_type=MESH)

    @pl.when(band < BANDS - 1)
    def _():
        pl.semaphore_signal(barrier, inc=1, device_id=(band + 1, group), device_id_type=MESH)


def meet(band):
    sides = (band > 0).astype(I32) + (band < BANDS - 1).astype(I32)
    pl.semaphore_wait(pltpu.get_barrier_semaphore(), GROUPS - 1 + sides)


def to_south(edge, landing, send_sem, recv_sem, index, band, group):
    return pltpu.make_async_remote_copy(
        src_ref=edge.at[index],
        dst_ref=landing.at[index],
        send_sem=send_sem.at[index],
        recv_sem=recv_sem.at[index],
        device_id=(jnp.maximum(band - 1, 0), group),
        device_id_type=MESH,
    )


def to_north(edge, landing, send_sem, recv_sem, index, band, group):
    return pltpu.make_async_remote_copy(
        src_ref=edge.at[index],
        dst_ref=landing.at[index],
        send_sem=send_sem.at[index],
        recv_sem=recv_sem.at[index],
        device_id=(jnp.minimum(band + 1, BANDS - 1), group),
        device_id_type=MESH,
    )


class Rims:
    def __init__(self, band, group, refs):
        self.band, self.group = band, group
        (
            self.edge_south,
            self.edge_north,
            self.halo_south,
            self.halo_north,
            self.send_south,
            self.send_north,
            self.recv_south,
            self.recv_north,
        ) = refs

    @staticmethod
    def scratch():
        steps = NT * LEVELS
        edges = pltpu.VMEM((steps + LEVELS, TILES, 128), F32)
        halos = pltpu.VMEM((steps, TILES, 128), F32)
        sems = pltpu.SemaphoreType.DMA((steps,))
        return [edges] * 2 + [halos] * 2 + [sems] * 4

    def clear(self):
        @pl.when(self.band == 0)
        def _():
            self.halo_south[...] = jnp.zeros_like(self.halo_south)

        @pl.when(self.band == BANDS - 1)
        def _():
            self.halo_north[...] = jnp.zeros_like(self.halo_north)

    def south(self, index):
        return to_south(
            self.edge_south, self.halo_north, self.send_south, self.recv_north,
            index, self.band, self.group,
        )

    def north(self, index):
        return to_north(
            self.edge_north, self.halo_south, self.send_north, self.recv_south,
            index, self.band, self.group,
        )

    def start(self, index):
        @pl.when(self.band > 0)
        def _():
            self.south(index).start()

        @pl.when(self.band < BANDS - 1)
        def _():
            self.north(index).start()

    def wait(self, index):
        @pl.when(self.band > 0)
        def _():
            self.north(index).wait_recv()

        @pl.when(self.band < BANDS - 1)
        def _():
            self.south(index).wait_recv()

    def drain(self):
        def one(index, carry):
            @pl.when(self.band > 0)
            def _():
                self.south(index).wait_send()

            @pl.when(self.band < BANDS - 1)
            def _():
                self.north(index).wait_send()

            return carry

        lax.fori_loop(0, NT * LEVELS, one, 0)


def for_peers(group, act):
    def one(step, carry):
        act(lax.rem(group + step, GROUPS))
        return carry

    lax.fori_loop(1, GROUPS, one, 0)


def forward_kernel(
    control_in, spread_in, vert_root_in, wind_lon_in, wind_lat_in, dest_in,
    cells_in, time_in, value_in, weight_in, rinv_in,
    states, received, rows, slots, wind_lon, wind_lat, dest,
    control, spread, vert_root, cells, time, value, weight, rinv, load_sems,
    increment, payload, field_send, field_recv, obs_send, obs_recv, *rim_refs,
):
    band, group = lax.axis_index("obs"), lax.axis_index("horiz")
    rims = Rims(band, group, rim_refs)
    loads = fetches(
        (
            control_in, vert_root_in, spread_in, dest_in, cells_in, time_in, value_in,
            weight_in, rinv_in, wind_lon_in, wind_lat_in,
        ),
        (
            control, vert_root, spread, dest, cells, time, value, weight, rinv,
            wind_lon, wind_lat,
        ),
        load_sems,
    )
    for load in loads:
        load.start()
    greet(band, group)
    rims.clear()
    for load in loads[:3]:
        load.wait()
    root = vert_root[...]
    for lat in range(8):
        column = control[:, lat, :]
        mixed = jnp.dot(
            root, column, precision=lax.Precision.HIGHEST, preferred_element_type=F32
        )
        increment[:, lat, :] = spread[:, lat, :] * mixed
    meet(band)

    def field_copy(target, source):
        return pltpu.make_async_remote_copy(
            src_ref=increment.at[pl.ds(LEVELS * target, LEVELS)],
            dst_ref=states.at[pl.ds(0, LEVELS), source],
            send_sem=field_send.at[target],
            recv_sem=field_recv.at[source],
            device_id=(band, target),
            device_id_type=MESH,
        )

    def obs_copy(target, source):
        return pltpu.make_async_remote_copy(
            src_ref=payload.at[target],
            dst_ref=received.at[source],
            send_sem=obs_send.at[target],
            recv_sem=obs_recv.at[source],
            device_id=(band, target),
            device_id_type=MESH,
        )

    for_peers(group, lambda peer: field_copy(peer, group).start())
    for level in range(LEVELS):
        states[level, group] = increment[LEVELS * group + level]

    for load in loads[3:]:
        load.wait()
    owner = dest[...]
    hit = lax.broadcasted_iota(I32, (GROUPS, 1024), 0) == owner
    hit_f = jnp.where(hit, 1.0, 0.0)
    hit_b = hit_f.astype(BF16)
    earlier = (
        lax.broadcasted_iota(I32, (128, 128), 0) < lax.broadcasted_iota(I32, (128, 128), 1)
    )
    earlier = jnp.where(earlier, 1.0, 0.0).astype(BF16)
    carried = jnp.zeros((GROUPS, 1), F32)
    for chunk in range(8):
        at = slice(chunk * 128, chunk * 128 + 128)
        before = jnp.dot(hit_b[:, at], earlier, preferred_element_type=F32) + carried
        slots[:, at] = jnp.sum(hit_f[:, at] * before, axis=0, keepdims=True).astype(I32)
        carried = carried + jnp.sum(hit_f[:, at], axis=1, keepdims=True)
    place = lax.broadcasted_iota(I32, (128, 1024), 0)
    slot_hit = (place & (CAP - 1)) == slots[...]
    first_half = place < CAP
    first_slot = jnp.logical_and(slot_hit, first_half)
    second_slot = jnp.logical_and(slot_hit, jnp.logical_not(first_half))
    fields = []
    for k in range(4):
        cell = cells[k : k + 1, :]
        row = (
            (time[...] * LEVELS + (cell >> 15)) * ROWS
            + ((cell & 4095) >> 7) * 8
            + ((cell >> 12) & 7)
        )
        fields.append(((row * 128 + (cell & 127)).astype(F32), weight[k : k + 1, :]))
    fields.append((value[...], rinv[...]))
    payload[...] = jnp.zeros_like(payload)
    for index, (first, second) in enumerate(fields):
        total = None
        for one, two in zip(split_three(first), split_three(second)):
            chosen = jnp.where(
                first_slot, one.astype(F32), jnp.where(second_slot, two.astype(F32), 0.0)
            ).astype(BF16)
            term = lax.dot_general(
                hit_b, chosen, (((1,), (1,)), ((), ())), preferred_element_type=F32
            )
            total = term if total is None else total + term
        payload[:, index, :] = total
    for_peers(group, lambda peer: obs_copy(peer, group).start())
    received[group] = payload[group]

    for_peers(group, lambda peer: field_copy(group, peer).wait_recv())
    for level in range(LEVELS):
        for tile in range(TILES):
            cell = states[level, tile]
            rims.edge_south[level, tile : tile + 1, :] = cell[0:1, :]
            rims.edge_north[level, tile : tile + 1, :] = cell[7:8, :]
        rims.start(level)

    lane = lax.broadcasted_iota(I32, (8, 128), 1)
    lat = lax.broadcasted_iota(I32, (8, 128), 0)

    def advance(index, carry):
        level = lax.rem(index, LEVELS)
        rims.wait(index)

        def tile_of(tile):
            now = states[index, tile % TILES]
            return now, pltpu.roll(now, 1, 1), pltpu.roll(now, 127, 1)

        before, here = tile_of(TILES - 1), tile_of(0)
        for tile in range(TILES):
            after = tile_of(tile + 1)
            now = here[0]
            west = jnp.where(lane == 0, before[1], here[1])
            east = jnp.where(lane == 127, after[2], here[2])
            south = jnp.where(
                lat == 0, rims.halo_south[index, tile : tile + 1, :], pltpu.roll(now, 1, 0)
            )
            north = jnp.where(
                lat == 7, rims.halo_north[index, tile : tile + 1, :], pltpu.roll(now, 7, 0)
            )
            at = slice(tile * 128, tile * 128 + 128)
            lon, lati = wind_lon[level, :, at], wind_lat[level, :, at]
            new = (
                now
                - jnp.maximum(lon, 0.0) * (now - west)
                - jnp.minimum(lon, 0.0) * (east - now)
                - jnp.maximum(lati, 0.0) * (now - south)
                - jnp.minimum(lati, 0.0) * (north - now)
            )
            states[index + LEVELS, tile] = new

            rims.edge_south[index + LEVELS, tile : tile + 1, :] = new[0:1, :]
            rims.edge_north[index + LEVELS, tile : tile + 1, :] = new[7:8, :]
            before, here = here, after

        @pl.when(index < (NT - 1) * LEVELS)
        def _():
            rims.start(index + LEVELS)

        return carry

    lax.fori_loop(0, NT * LEVELS, advance, 0)

    for_peers(group, lambda peer: obs_copy(group, peer).wait_recv())
    for sender in range(GROUPS):
        rows[sender * 8 : sender * 8 + 8, :] = received[sender].astype(I32) >> 7
    for_peers(group, lambda peer: field_copy(peer, group).wait_send())
    for_peers(group, lambda peer: obs_copy(peer, group).wait_send())
    rims.drain()


def obs_kernel(rows, received, states, forcing, departure, picked, placed, *sums):
    for one in sums:
        one[...] = jnp.zeros_like(one)
    lane = lax.broadcasted_iota(I32, (CAP, 128), 1)
    place = lax.broadcasted_iota(I32, (CAP, 128), 0)

    def block(sender, carry):
        flipped = received[sender].T
        for k in range(4):
            for s in range(CAP):
                row = rows[sender * 8 + k, s]
                picked[k * CAP + s : k * CAP + s + 1, :] = states[pl.ds(row, 1), :]
        hits, total = [], None
        for k in range(4):
            where = flipped[0:CAP, k : k + 1].astype(I32) & 127
            hits.append(jnp.where(lane == where, flipped[CAP:, k : k + 1], 0.0))
            term = hits[k] * picked[k * CAP : k * CAP + CAP, :]
            total = term if total is None else total + term
        hx = jnp.sum(total, axis=1, keepdims=True)
        weighted = flipped[CAP:, 4:5] * (hx - flipped[0:CAP, 4:5])
        for k in range(4):
            placed[k * CAP : k * CAP + CAP, :] = hits[k] * weighted
        departure[sender] = jnp.sum(
            jnp.where(lane == place, weighted, 0.0), axis=0, keepdims=True
        )
        for s in range(CAP):
            for k in range(4):
                one = sums[(s * 4 + k) % ACCS]
                row = rows[sender * 8 + k, s]
                one[pl.ds(row, 1), :] += placed[k * CAP + s : k * CAP + s + 1, :]
        return carry

    lax.fori_loop(0, GROUPS, block, 0)

    def add(index, carry):
        at = pl.ds(pl.multiple_of(index * 64, 64), 64)
        total = sums[0][at, :]
        for one in sums[1:]:
            total = total + one[at, :]
        forcing[at, :] = total
        return carry

    lax.fori_loop(0, (NT + 1) * LEVELS * ROWS // 64, add, 0)


def adjoint_kernel(
    control_in, spread_in, vert_root_in, wind_lon, wind_lat, forcing, owner_dep, dest, slots,
    gradient, departure,
    control, spread, vert_root, load_sems,
    adjoint, column, returned, field_send, field_recv, dep_send, dep_recv, *rim_refs,
):
    band, group = lax.axis_index("obs"), lax.axis_index("horiz")
    rims = Rims(band, group, rim_refs)
    loads = fetches(
        (control_in, spread_in, vert_root_in), (control, spread, vert_root), load_sems
    )
    for load in loads:
        load.start()
    greet(band, group)
    rims.clear()
    for level in range(LEVELS):
        for tile in range(TILES):
            at = slice(tile * 128, tile * 128 + 128)
            now = forcing[NT * LEVELS + level, tile]
            lati = wind_lat[level, :, at]
            adjoint[level, tile] = now
            rims.edge_south[level, tile : tile + 1, :] = (jnp.maximum(lati, 0.0) * now)[0:1, :]
            rims.edge_north[level, tile : tile + 1, :] = (jnp.minimum(lati, 0.0) * now)[7:8, :]
    meet(band)
    for level in range(LEVELS):
        rims.start(level)

    def dep_copy(target, source):
        return pltpu.make_async_remote_copy(
            src_ref=owner_dep.at[target],
            dst_ref=returned.at[source],
            send_sem=dep_send.at[target],
            recv_sem=dep_recv.at[source],
            device_id=(band, target),
            device_id_type=MESH,
        )

    def field_copy(target, source):
        return pltpu.make_async_remote_copy(
            src_ref=adjoint.at[pl.ds(NT * LEVELS, LEVELS), target],
            dst_ref=column.at[pl.ds(LEVELS * source, LEVELS)],
            send_sem=field_send.at[target],
            recv_sem=field_recv.at[source],
            device_id=(band, target),
            device_id_type=MESH,
        )

    for_peers(group, lambda peer: dep_copy(peer, group).start())
    returned[group] = owner_dep[group]

    lane = lax.broadcasted_iota(I32, (8, 128), 1)
    lat = lax.broadcasted_iota(I32, (8, 128), 0)

    def retreat(index, carry):
        level = lax.rem(index, LEVELS)
        step = lax.div(index, LEVELS)
        rims.wait(index)

        def tile_of(tile):
            tile = tile % TILES
            at = slice(tile * 128, tile * 128 + 128)
            now = adjoint[index, tile]
            lon = wind_lon[level, :, at]
            up, down = jnp.maximum(lon, 0.0), jnp.minimum(lon, 0.0)
            return (
                now,
                1.0 - up + down,
                pltpu.roll(up * now, 127, 1),
                pltpu.roll(down * now, 1, 1),
            )

        before, here = tile_of(TILES - 1), tile_of(0)
        for tile in range(TILES):
            after = tile_of(tile + 1)
            at = slice(tile * 128, tile * 128 + 128)
            now = here[0]
            lati = wind_lat[level, :, at]
            up, down = jnp.maximum(lati, 0.0), jnp.minimum(lati, 0.0)
            from_east = jnp.where(lane == 127, after[2], here[2])
            from_west = jnp.where(lane == 0, before[3], here[3])
            from_north = jnp.where(
                lat == 7, rims.halo_north[index, tile : tile + 1, :], pltpu.roll(up * now, 7, 0)
            )
            from_south = jnp.where(
                lat == 0, rims.halo_south[index, tile : tile + 1, :], pltpu.roll(down * now, 1, 0)
            )
            new = (
                (here[1] - up + down) * now
                + from_east
                - from_west
                + from_north
                - from_south
                + forcing[(NT - 1 - step) * LEVELS + level, tile]
            )
            adjoint[index + LEVELS, tile] = new

            rims.edge_south[index + LEVELS, tile : tile + 1, :] = (up * new)[0:1, :]
            rims.edge_north[index + LEVELS, tile : tile + 1, :] = (down * new)[7:8, :]
            before, here = here, after

        @pl.when(index < (NT - 1) * LEVELS)
        def _():
            rims.start(index + LEVELS)

        return carry

    lax.fori_loop(0, NT * LEVELS, retreat, 0)

    for_peers(group, lambda peer: field_copy(peer, group).start())
    for level in range(LEVELS):
        column[LEVELS * group + level] = adjoint[NT * LEVELS + level, group]

    for_peers(group, lambda peer: dep_copy(group, peer).wait_recv())
    hit = lax.broadcasted_iota(I32, (GROUPS, 1024), 0) == dest[...]
    hit = jnp.where(hit, 1.0, 0.0).astype(BF16)
    spread_out = None
    for part in split_three(returned[:, 0, :]):
        term = lax.dot_general(
            part, hit, (((0,), (0,)), ((), ())), preferred_element_type=F32
        )
        spread_out = term if spread_out is None else spread_out + term
    place = lax.broadcasted_iota(I32, (128, 1024), 0)
    departure[...] = jnp.sum(
        jnp.where(place == slots[...], spread_out, 0.0), axis=0, keepdims=True
    )

    for load in loads:
        load.wait()
    root = vert_root[...].T
    for_peers(group, lambda peer: field_copy(group, peer).wait_recv())
    for lat_row in range(8):
        weighted = spread[:, lat_row, :] * column[:, lat_row, :]
        mixed = jnp.dot(
            root, weighted, precision=lax.Precision.HIGHEST, preferred_element_type=F32
        )
        gradient[:, lat_row, :] = control[:, lat_row, :] + mixed
    for_peers(group, lambda peer: field_copy(peer, group).wait_send())
    for_peers(group, lambda peer: dep_copy(peer, group).wait_send())
    rims.drain()


def per_device(
    control, spread, vert_root, wind_lon, wind_lat,
    obs_dest, obs_cells, obs_time, obs_value, obs_weight, obs_rinv,
):
    count = obs_time.shape[0]
    dest = obs_dest.reshape(1, count)
    fields = (NT + 1) * LEVELS
    wide, long = control.shape, (LEVELS, 8, TILES * 128)
    states, received, rows, slots, lon, lat, owner = pl.pallas_call(
        forward_kernel,
        out_shape=(
            jax.ShapeDtypeStruct((fields, TILES, 8, 128), F32),
            jax.ShapeDtypeStruct((GROUPS, 8, 128), F32),
            jax.ShapeDtypeStruct((GROUPS * 8, 128), I32),
            jax.ShapeDtypeStruct((1, count), I32),
            jax.ShapeDtypeStruct(long, F32),
            jax.ShapeDtypeStruct(long, F32),
            jax.ShapeDtypeStruct((1, count), I32),
        ),
        in_specs=[in_hbm()] * 11,
        out_specs=(in_vmem(),) * 7,
        scratch_shapes=[
            pltpu.VMEM(wide, F32),
            pltpu.VMEM(wide, F32),
            pltpu.VMEM((128, 128), F32),
            pltpu.VMEM((4, count), I32),
            pltpu.VMEM((1, count), I32),
            pltpu.VMEM((1, count), F32),
            pltpu.VMEM((4, count), F32),
            pltpu.VMEM((1, count), F32),
            pltpu.SemaphoreType.DMA((11,)),
            pltpu.VMEM(wide, F32),
            pltpu.VMEM((GROUPS, 8, 128), F32),
        ]
        + [pltpu.SemaphoreType.DMA((GROUPS,))] * 4
        + Rims.scratch(),
        compiler_params=pltpu.CompilerParams(
            collective_id=0, has_side_effects=True, vmem_limit_bytes=48 << 20
        ),
        name="forward",
    )(
        control, spread, vert_root, wind_lon, wind_lat, dest, obs_cells,
        obs_time.reshape(1, count), obs_value.reshape(1, count), obs_weight,
        obs_rinv.reshape(1, count),
    )
    forcing, owner_dep = pl.pallas_call(
        obs_kernel,
        out_shape=(
            jax.ShapeDtypeStruct((fields * ROWS, 128), F32),
            jax.ShapeDtypeStruct((GROUPS, 1, 128), F32),
        ),
        in_specs=[pl.BlockSpec(memory_space=pltpu.SMEM), in_vmem(), in_vmem()],
        out_specs=(in_vmem(),) * 2,
        scratch_shapes=[pltpu.VMEM((4 * CAP, 128), F32)] * 2
        + [pltpu.VMEM((fields * ROWS, 128), F32)] * ACCS,
        compiler_params=pltpu.CompilerParams(vmem_limit_bytes=48 << 20),
        name="observe",
    )(rows, received, states.reshape(fields * ROWS, 128))
    gradient, departure = pl.pallas_call(
        adjoint_kernel,
        out_shape=(
            jax.ShapeDtypeStruct(control.shape, F32),
            jax.ShapeDtypeStruct((1, count), F32),
        ),
        in_specs=[in_hbm()] * 3 + [in_vmem()] * 6,
        out_specs=(in_vmem(),) * 2,
        scratch_shapes=[
            pltpu.VMEM(wide, F32),
            pltpu.VMEM(wide, F32),
            pltpu.VMEM((128, 128), F32),
            pltpu.SemaphoreType.DMA((3,)),
            pltpu.VMEM((fields, TILES, 8, 128), F32),
            pltpu.VMEM((128, 8, 128), F32),
            pltpu.VMEM((GROUPS, 1, 128), F32),
        ]
        + [pltpu.SemaphoreType.DMA((GROUPS,))] * 4
        + Rims.scratch(),
        compiler_params=pltpu.CompilerParams(
            collective_id=1, has_side_effects=True, vmem_limit_bytes=48 << 20
        ),
        name="retreat",
    )(
        control, spread, vert_root, lon, lat,
        forcing.reshape(fields, TILES, 8, 128), owner_dep, owner, slots,
    )
    return gradient, departure.reshape(count)


def solution(mesh):
    in_specs = (
        P(None, "obs", "horiz"),
        P(None, "obs", "horiz"),
        P(),
        P("horiz", "obs", None),
        P("horiz", "obs", None),
        P(("obs", "horiz"), None),
        P(None, ("obs", "horiz")),
        P(("obs", "horiz")),
        P(("obs", "horiz")),
        P(None, ("obs", "horiz")),
        P(("obs", "horiz")),
    )
    out_specs = (P(None, "obs", "horiz"), P(("obs", "horiz")))
    return jax.shard_map(
        per_device, mesh=mesh, in_specs=in_specs, out_specs=out_specs, check_vma=False
    )
```

time: 337 us -> 108 us (0.32)
  other arithmetic: 100 us -> 0 us
  Pallas kernels: 0 us -> 95.1 us
  local copies, waits for them, and re-layouts: 98.3 us -> 10.6 us
  starting transfers between devices: 76.3 us -> 0 us
  waiting for transfers between devices: 46.6 us -> 0 us
  matrix products: 12.3 us -> 0 us
    pallas_call x0 -> x3, Pallas kernels: none -> 95.1 us  [the longest x1 34.5 us: per_device(): pl.pallas_call(forward_kernel, out_shape=(jax.ShapeDtypeStruct((fields, T...]
    scatter-add x1 -> x0, other arithmetic: 57 us -> none  [per_device(): jnp.zeros(states_rows.shape, jnp.float32).at[row_ids.reshape(-1)]]
    ppermute x16 -> x0, starting transfers between devices: 43.9 us -> none  [the longest x8 26.1 us: padded_2(): lax.ppermute(tail, axis, [(i, (i + 1) % count) for i in range(ends)])]
    all_to_all x5 -> x0, starting transfers between devices: 32.4 us -> none  [the longest x1 8.41 us: per_device(): lax.all_to_all(int_buffer, 'horiz', split_axis=1, concat_axis=1, tiled=True)]
    ppermute x16 -> x0, waiting for transfers between devices: 29.4 us -> none  [the longest x8 29.4 us: padded_2(): lax.ppermute(head, axis, [((i + 1) % count, i) for i in range(ends)])]
    gather x1 -> x0, local copies, waits for them, and re-layouts: 27.8 us -> none  [per_device(): picked = jnp.sum(states_rows[row_ids] * lane_hit, axis=2)]
    unnamed x52 -> x24, local copies, waits for them, and re-layouts: 30 us -> 10.6 us
    all_to_all x5 -> x0, waiting for transfers between devices: 17.2 us -> none  [the longest x1 6.62 us: per_device(): lax.all_to_all(increment, 'horiz', split_axis=0, concat_axis=2, tiled=True)]
  transfers between devices with their start and end apart: 21 -> 0, of which waited for: 11 -> 0; matrix products, arithmetic and copies ran while one was open for 15% -> 0% of each run, Pallas kernels for 0% -> 0%
where the time goes in v1:
time: 108 us; the launch traced here: 106 us
  Pallas kernels  95.1 us (88%)
  local copies, waits for them, and re-layouts  10.6 us (10%)
    pallas_call x1, Pallas kernels, per_device(): pl.pallas_call(forward_kernel, out_shape=(jax.ShapeDtypeStruct((fields, T...  34.5 us
    pallas_call x1, Pallas kernels, per_device(): pl.pallas_call(adjoint_kernel, out_shape=(jax.ShapeDtypeStruct(control.sh...  32.1 us
    pallas_call x1, Pallas kernels, per_device(): pl.pallas_call(obs_kernel, out_shape=(jax.ShapeDtypeStruct((fields * ROWS...  28.5 us
    unnamed x24, local copies, waits for them, and re-layouts  10.6 us

profile of v1, /device:TPU:67, one launch (start us, length us, event | category | flops | bytes accessed | tf_op | source)
XLA Modules:
  0.0 106.4 jit_solution(2989337564663665909)
XLA Ops:
  0.6 0.0 copy-start
  0.6 1.0 copy-done
  1.7 0.0 copy-start.1
  1.7 1.0 copy-done.1
  2.7 0.0 copy-start.2
  2.7 1.0 copy-done.2
  3.8 0.0 copy-start.3
  3.8 1.0 copy-done.3
  4.8 0.0 copy-start.4
  4.8 0.8 copy-done.4
  5.6 0.0 copy-start.5
  5.6 0.7 copy-done.5
  6.4 0.0 copy-start.6
  6.4 0.7 copy-done.6
  7.1 0.0 copy-start.7
  7.1 0.7 copy-done.7
  7.8 0.7 copy-done.8
  8.5 0.7 copy-done.9
  9.1 0.7 copy-done.10
  9.8 34.5 %forward.1 = (f32[20,32,8,128]{3,2,1,0:T(8,128)S(1)}, f32[32,8,128]{2,1,0:T(8,128)S(1)}, s32[256,128]{1,0:T(8,128)S(1)}, s32[1,1024]{1,0:T(1,128)S(1)}, f32[4,8,...) custom-call(f32[128,8,128]{2,1,0:T(8,128)S(1)} %copy-done, f32[128,8,128]{2,1,0:T(8,128)S(1)} %copy-done.1, ...), custom_call_target="tpu_custom_call" | custom-call | tf_op jit(solution)/shard_map/forward/pallas_call | solution.py:536
  44.4 28.5 %observe.1 = (f32[5120,128]{1,0:T(8,128)S(1)}, f32[32,1,128]{2,1,0:T(1,128)S(1)}) custom-call(s32[256,128]{1,0:T(8,128)S(1)} %get-tuple-element.15.rows, f32[32,8,128]{2,1,0:T(8,128)S(1)} %get-tuple-element.16.received, f32[5120,128]{1,0:T(8,128)S(1)} %bitcast.8), custom_call_target="tpu_custom_call" | custom-call | tf_op jit(solution)/shard_map/observe/pallas_call | solution.py:573
  72.9 32.1 %retreat.1 = (f32[128,8,128]{2,1,0:T(8,128)S(1)}, f32[1,1024]{1,0:T(1,128)S(1)}) custom-call(f32[128,8,128]{2,1,0:T(8,128)S(1)} %copy-done, f32[128,8,128]{2,1,0:T(8,128)S(1)} %copy-done.1, f32[128,128]{1,0:T(8,128)S(1)} %copy-done.4, f32[4,8,4096]{2,1,0:T(8,128)S(1)} %get-tuple-element.13.wind_lon, f32[4,8,4096]{2,1,0:T(8,128)S(1)} %get-tuple-element.14.wind_lat, ...), custom_call_target="tpu_custom_call" | custom-call | tf_op jit(solution)/shard_map/retreat/pallas_call | solution.py:586
  105.0 0.8 copy.15
  105.8 0.6 copy.16
  (3 shorter events, 0.0 us)
Async XLA Ops:
  0.6 1.0 copy-start
  1.7 1.0 copy-start.1
  2.7 1.0 copy-start.2
  3.8 1.0 copy-start.3
  4.8 0.8 copy-start.4
  5.6 0.7 copy-start.5
  6.4 0.7 copy-start.6
  7.1 0.7 copy-start.7
  7.8 0.7 copy-start.8
  8.5 0.7 copy-start.9
  9.1 0.7 copy-start.10

commit v2 on v1

--- a/solution.py
+++ b/solution.py
@@ -25,6 +25,10 @@
 
 def in_hbm():
     return pl.BlockSpec(memory_space=pltpu.HBM)
+
+
+def stay(x):
+    return pltpu.with_memory_space_constraint(x, pltpu.HBM)
 
 
 def fetches(sources, targets, sems):
@@ -339,18 +343,29 @@
     rims.drain()
 
 
-def obs_kernel(rows, received, states, forcing, departure, picked, placed, *sums):
-    for one in sums:
-        one[...] = jnp.zeros_like(one)
+def obs_kernel(
+    rows, received, states, forcing, departure, picked, placed, indices, index_sems, *sums
+):
     lane = lax.broadcasted_iota(I32, (CAP, 128), 1)
     place = lax.broadcasted_iota(I32, (CAP, 128), 0)
-
-    def block(sender, carry):
+    size = 4 * CAP
+
+    def fetch(sender, side):
+        at = pl.ds(pl.multiple_of(jnp.minimum(sender, GROUPS - 1) * 8, 8), 8)
+        return pltpu.make_async_copy(rows.at[at], indices.at[side], index_sems.at[side])
+
+    def gather(k, s, side):
+        row = indices[side, k, s]
+        picked[k * CAP + s : k * CAP + s + 1, :] = states[pl.ds(row, 1), :]
+
+    def scatter(k, s, side):
+        one = sums[(s * 4 + k) % ACCS]
+        at = (side % 2) * size + k * CAP + s
+        row = indices[side, k, s]
+        one[pl.ds(row, 1), :] += placed[at : at + 1, :]
+
+    def weigh(sender, side):
         flipped = received[sender].T
-        for k in range(4):
-            for s in range(CAP):
-                row = rows[sender * 8 + k, s]
-                picked[k * CAP + s : k * CAP + s + 1, :] = states[pl.ds(row, 1), :]
         hits, total = [], None
         for k in range(4):
             where = flipped[0:CAP, k : k + 1].astype(I32) & 127
@@ -360,18 +375,37 @@
         hx = jnp.sum(total, axis=1, keepdims=True)
         weighted = flipped[CAP:, 4:5] * (hx - flipped[0:CAP, 4:5])
         for k in range(4):
-            placed[k * CAP : k * CAP + CAP, :] = hits[k] * weighted
+            at = (side % 2) * size + k * CAP
+            placed[at : at + CAP, :] = hits[k] * weighted
         departure[sender] = jnp.sum(
             jnp.where(lane == place, weighted, 0.0), axis=0, keepdims=True
         )
-        for s in range(CAP):
-            for k in range(4):
-                one = sums[(s * 4 + k) % ACCS]
-                row = rows[sender * 8 + k, s]
-                one[pl.ds(row, 1), :] += placed[k * CAP + s : k * CAP + s + 1, :]
+
+    for side in range(4):
+        fetch(side, side).start()
+    for one in sums:
+        one[...] = jnp.zeros_like(one)
+    fetch(0, 0).wait()
+    for s in range(CAP):
+        for k in range(4):
+            gather(k, s, 0)
+    weigh(0, 0)
+
+    def four(index, carry):
+        for side in range(4):
+            sender, ahead = 4 * index + side, (side + 1) % 4
+            fetch(sender + 1, ahead).wait()
+            for s in range(CAP):
+                for k in range(4):
+                    gather(k, s, ahead)
+                    scatter(k, s, side)
+            weigh(jnp.minimum(sender + 1, GROUPS - 1), ahead)
+            fetch(sender + 4, side).start()
         return carry
 
-    lax.fori_loop(0, GROUPS, block, 0)
+    lax.fori_loop(0, GROUPS // 4, four, 0)
+    for side in range(1, 4):
+        fetch(GROUPS + side, side).wait()
 
     def add(index, carry):
         at = pl.ds(pl.multiple_of(index * 64, 64), 64)
@@ -566,9 +600,11 @@
         ),
         name="forward",
     )(
-        control, spread, vert_root, wind_lon, wind_lat, dest, obs_cells,
-        obs_time.reshape(1, count), obs_value.reshape(1, count), obs_weight,
-        obs_rinv.reshape(1, count),
+        *map(stay, (
+            control, spread, vert_root, wind_lon, wind_lat, dest, obs_cells,
+            obs_time.reshape(1, count), obs_value.reshape(1, count), obs_weight,
+            obs_rinv.reshape(1, count),
+        ))
     )
     forcing, owner_dep = pl.pallas_call(
         obs_kernel,
@@ -576,9 +612,14 @@
             jax.ShapeDtypeStruct((fields * ROWS, 128), F32),
             jax.ShapeDtypeStruct((GROUPS, 1, 128), F32),
         ),
-        in_specs=[pl.BlockSpec(memory_space=pltpu.SMEM), in_vmem(), in_vmem()],
+        in_specs=[in_vmem()] * 3,
         out_specs=(in_vmem(),) * 2,
-        scratch_shapes=[pltpu.VMEM((4 * CAP, 128), F32)] * 2
+        scratch_shapes=[
+            pltpu.VMEM((4 * CAP, 128), F32),
+            pltpu.VMEM((8 * CAP, 128), F32),
+            pltpu.SMEM((4, 8, 128), I32),
+            pltpu.SemaphoreType.DMA((4,)),
+        ]
         + [pltpu.VMEM((fields * ROWS, 128), F32)] * ACCS,
         compiler_params=pltpu.CompilerParams(vmem_limit_bytes=48 << 20),
         name="observe",
@@ -607,7 +648,7 @@
         ),
         name="retreat",
     )(
-        control, spread, vert_root, lon, lat,
+        stay(control), stay(spread), stay(vert_root), lon, lat,
         forcing.reshape(fields, TILES, 8, 128), owner_dep, owner, slots,
     )
     return gradient, departure.reshape(count)

time: 108 us -> 89.5 us (0.83)
  local copies, waits for them, and re-layouts: 10.6 us -> 1.39 us
  Pallas kernels: 95.1 us -> 86.8 us
    unnamed x24 -> x2, local copies, waits for them, and re-layouts: 10.6 us -> 1.39 us
    pallas_call x1, Pallas kernels: 28.5 us -> 20.3 us  [per_device(): pl.pallas_call(obs_kernel, out_shape=(jax.ShapeDtypeStruct((fields * ROWS...]
where the time goes in v2:
time: 89.5 us; the launch traced here: 88.8 us
  Pallas kernels  86.8 us (97%)
  local copies, waits for them, and re-layouts  1.39 us (2%)
    pallas_call x1, Pallas kernels, per_device(): pl.pallas_call(forward_kernel, out_shape=(jax.ShapeDtypeStruct((fields, T...  34.4 us
    pallas_call x1, Pallas kernels, per_device(): pl.pallas_call(adjoint_kernel, out_shape=(jax.ShapeDtypeStruct(control.sh...  32 us
    pallas_call x1, Pallas kernels, per_device(): pl.pallas_call(obs_kernel, out_shape=(jax.ShapeDtypeStruct((fields * ROWS...  20.3 us

profile of v2, /device:TPU:67, one launch (start us, length us, event | category | flops | bytes accessed | tf_op | source)
XLA Modules:
  0.0 88.8 jit_solution(7930724503860021462)
XLA Ops:
  0.6 34.4 %forward.1 = (f32[20,32,8,128]{3,2,1,0:T(8,128)S(1)}, f32[32,8,128]{2,1,0:T(8,128)S(1)}, s32[256,128]{1,0:T(8,128)S(1)}, s32[1,1024]{1,0:T(1,128)S(1)}, f32[4,8,...) custom-call(f32[128,8,128]{2,1,0:T(8,128)} %control_in.3, f32[128,8,128]{2,1,0:T(8,128)} %spread_in.3, ...), custom_call_target="tpu_custom_call" | custom-call | tf_op jit(solution)/shard_map/forward/pallas_call | solution.py:570
  35.1 20.3 %observe.1 = (f32[5120,128]{1,0:T(8,128)S(1)}, f32[32,1,128]{2,1,0:T(1,128)S(1)}) custom-call(s32[256,128]{1,0:T(8,128)S(1)} %get-tuple-element.15.rows, f32[32,8,128]{2,1,0:T(8,128)S(1)} %get-tuple-element.16.received, f32[5120,128]{1,0:T(8,128)S(1)} %bitcast.8), custom_call_target="tpu_custom_call" | custom-call | tf_op jit(solution)/shard_map/observe/pallas_call | solution.py:609
  55.4 32.0 %retreat.1 = (f32[128,8,128]{2,1,0:T(8,128)S(1)}, f32[1,1024]{1,0:T(1,128)S(1)}) custom-call(f32[128,8,128]{2,1,0:T(8,128)} %control_in.3, f32[128,8,128]{2,1,0:T(8,128)} %spread_in.3, f32[128,128]{1,0:T(8,128)} %vert_root_in.3, f32[4,8,4096]{2,1,0:T(8,128)S(1)} %get-tuple-element.13.wind_lon, f32[4,8,4096]{2,1,0:T(8,128)S(1)} %get-tuple-element.14.wind_lat, ...), custom_call_target="tpu_custom_call" | custom-call | tf_op jit(solution)/shard_map/retreat/pallas_call | solution.py:627
  87.4 0.8 copy.15
  88.2 0.6 copy.16
